TPU v7x, 32 devices: a whole 2x2x4 slice. The times are simulated.
32 devices in a mesh: groups: 2 (over y), head: 8 (over z, x), blk: 2 (over core).
Axes of the slice: x: 2, y: 2, z: 4, core: 2. Of those that a mesh axis runs over, the one named last changes fastest.
Arguments:
- queries: bfloat16 [1024, 2048], P(('groups', 'head', 'blk')), parts along dimension 0, may hold values from -6 to 6
- key_rows: bfloat16 [1024, 256], P(('groups', 'head', 'blk')), parts along dimension 0, may hold values from -6 to 6
- value_rows: bfloat16 [1024, 256], P(('groups', 'head', 'blk')), parts along dimension 0, may hold values from -6 to 6
- fwd_output: bfloat16 [1024, 2048], P(('groups', 'head', 'blk')), parts along dimension 0, may hold values from -6 to 6
- grad_out: bfloat16 [1024, 2048], P(('groups', 'head', 'blk')), parts along dimension 0, may hold values from -6 to 6
- log_norm: float32 [1024, 16], P(('groups', 'head', 'blk')), parts along dimension 0, may hold values from 2 to 5.5
- visible: int32 [8, 4], P('groups'), parts along dimension 0, may hold values from 0 to 1, as said below
- seg_lengths: int32 [8], P('groups'), parts along dimension 0, may hold values from 1 to 256, 512 in all
Outputs:
- grad_queries: bfloat16 [1024, 2048], P(('groups', 'head', 'blk')), parts along dimension 0
- grad_keys: bfloat16 [1024, 256], P(('groups', 'head', 'blk')), parts along dimension 0
- grad_values: bfloat16 [1024, 256], P(('groups', 'head', 'blk')), parts along dimension 0
There are 2 independent parts, one for each index of `groups`. A program takes and returns all parts, laid end to end along the dimension named above; each array names one. Nothing has to cross between parts.
Inputs may be any that keep to these rules, and one draw needn't show every extreme that they name: visible[a, b] is 1 exactly when block b is block a or an ancestor of block a in a tree over the 4 blocks whose root is block 0 and in which every block's parent comes before it.
All inputs are finite; a program needn't handle non-finite values.
Results may differ from a plain program's by a relative error of at most 0.0051.
Values may be sent and summed in bfloat16 or wider, within the bound.
A program may use at most 64 MiB of HBM per device.

v0:
```python
import math

import jax
import jax.numpy as jnp
from jax import lax
from jax.sharding import PartitionSpec as P

BLOCK = 128


top_precision = lax.Precision.HIGHEST


def from_behind(value, axis, steps):
    count = lax.axis_size(axis)
    pairs = [(source, (source + steps) % count) for source in range(count)]
    return lax.ppermute(value, axis, pairs)


def token_spots(row_count, tok_rows, cycle_size, cycle_owner):
    iota_rows = jnp.arange(row_count, dtype=jnp.int32)
    return (
        iota_rows // tok_rows * (cycle_size * tok_rows)
        + cycle_owner * tok_rows
        + iota_rows % tok_rows
    )


def allowed_pairs(query_pos, key_pos, visible_f, seg_ends):
    block_iota = jnp.arange(visible_f.shape[0], dtype=jnp.int32)
    query_block = query_pos // BLOCK
    key_block = key_pos // BLOCK
    query_hot = (query_block[:, None] == block_iota[None, :]).astype(jnp.float32)
    key_hot = (key_block[:, None] == block_iota[None, :]).astype(jnp.float32)
    reach_rows = jnp.dot(query_hot, visible_f, precision=top_precision)
    reach_table = jnp.dot(reach_rows, key_hot.T, precision=top_precision)
    query_doc = jnp.sum((query_pos[:, None] >= seg_ends[None, :]).astype(jnp.int32), axis=1)
    key_doc = jnp.sum((key_pos[:, None] >= seg_ends[None, :]).astype(jnp.int32), axis=1)
    earlier = (query_block[:, None] != key_block[None, :]) | (
        key_pos[None, :] <= query_pos[:, None]
    )
    return (reach_table > 0.5) & (query_doc[:, None] == key_doc[None, :]) & earlier


def tile_grads(query_part, grad_rows, lse_rows, delta_rows, key_part, value_part, allowed):
    softmax_scale = 1.0 / math.sqrt(query_part.shape[2])
    scores = (
        jnp.einsum("qhd,khd->hqk", query_part, key_part, preferred_element_type=jnp.float32)
        * softmax_scale
    )
    prob_full = jnp.where(allowed[None], jnp.exp(scores - lse_rows.T[:, :, None]), 0.0)
    prob_half = prob_full.astype(jnp.bfloat16)
    value_grad = jnp.einsum(
        "hqk,qhd->khd", prob_half, grad_rows, preferred_element_type=jnp.float32
    )
    grad_prob = jnp.einsum(
        "qhd,khd->hqk", grad_rows, value_part, preferred_element_type=jnp.float32
    )
    grad_score = (prob_full * (grad_prob - delta_rows.T[:, :, None]) * softmax_scale).astype(
        jnp.bfloat16
    )
    query_grad = jnp.einsum(
        "hqk,khd->qhd", grad_score, key_part, preferred_element_type=jnp.float32
    )
    key_grad = jnp.einsum(
        "hqk,qhd->khd", grad_score, query_part, preferred_element_type=jnp.float32
    )
    return (query_grad, key_grad, value_grad)


def shards(queries, key_rows, value_rows, fwd_output, grad_out, log_norm, visible, seg_lengths):
    tok_rows, model_width = queries.shape
    head_total = log_norm.shape[1]
    head_dim = model_width // head_total
    kv_total = key_rows.shape[1] // head_dim
    group_size = head_total // kv_total
    query_heads = queries.reshape(tok_rows, head_total, head_dim)
    grad_heads = grad_out.reshape(tok_rows, head_total, head_dim)
    out_heads = fwd_output.reshape(tok_rows, head_total, head_dim)
    row_delta = jnp.sum(grad_heads.astype(jnp.float32) * out_heads.astype(jnp.float32), axis=2)
    key_heads = jnp.repeat(key_rows.reshape(tok_rows, kv_total, head_dim), group_size, axis=1)
    value_heads = jnp.repeat(value_rows.reshape(tok_rows, kv_total, head_dim), group_size, axis=1)
    local_q, local_g, local_k, local_v = (
        lax.all_to_all(query_heads, "head", split_axis=1, concat_axis=0, tiled=True),
        lax.all_to_all(grad_heads, "head", split_axis=1, concat_axis=0, tiled=True),
        lax.all_to_all(key_heads, "head", split_axis=1, concat_axis=0, tiled=True),
        lax.all_to_all(value_heads, "head", split_axis=1, concat_axis=0, tiled=True),
    )
    local_lse, local_delta = (
        lax.all_to_all(log_norm, "head", split_axis=1, concat_axis=0, tiled=True),
        lax.all_to_all(row_delta, "head", split_axis=1, concat_axis=0, tiled=True),
    )
    row_count = local_q.shape[0]
    cycle_size = lax.axis_size("blk")
    cycle_owner = lax.axis_index("blk")
    query_pos = token_spots(row_count, tok_rows, cycle_size, cycle_owner)
    visible_f = visible.astype(jnp.float32)
    seg_ends = jnp.cumsum(seg_lengths)

    def pair_grads(key_part, value_part, source):
        key_pos = token_spots(row_count, tok_rows, cycle_size, source)
        allowed = allowed_pairs(query_pos, key_pos, visible_f, seg_ends)
        return tile_grads(local_q, local_g, local_lse, local_delta, key_part, value_part, allowed)

    zero_grads = jnp.zeros(local_k.shape, jnp.float32)

    def one_turn(turn_index, carry_state):
        key_now, value_now, key_acc, value_acc, query_acc = carry_state
        source = (cycle_owner - turn_index) % cycle_size
        query_part, key_part, value_part = pair_grads(key_now, value_now, source)
        key_now, value_now = from_behind((key_now, value_now), "blk", 1)
        key_acc, value_acc = from_behind((key_acc + key_part, value_acc + value_part), "blk", 1)
        return (key_now, value_now, key_acc, value_acc, query_acc + query_part)

    start_state = (local_k, local_v, zero_grads, zero_grads, zero_grads)
    final_state = lax.fori_loop(0, cycle_size, one_turn, start_state)
    key_grad, value_grad, query_grad = (final_state[2], final_state[3], final_state[4])
    query_home = lax.all_to_all(
        query_grad.astype(jnp.bfloat16), "head", split_axis=0, concat_axis=1, tiled=True
    )
    grad_queries = query_home.reshape(tok_rows, model_width)
    key_home, value_home = (
        lax.all_to_all(key_grad, "head", split_axis=0, concat_axis=1, tiled=True),
        lax.all_to_all(value_grad, "head", split_axis=0, concat_axis=1, tiled=True),
    )
    key_total = jnp.sum(key_home.reshape(tok_rows, kv_total, group_size, head_dim), axis=2)
    value_total = jnp.sum(value_home.reshape(tok_rows, kv_total, group_size, head_dim), axis=2)
    grad_keys = key_total.reshape(tok_rows, kv_total * head_dim).astype(jnp.bfloat16)
    grad_values = value_total.reshape(tok_rows, kv_total * head_dim).astype(jnp.bfloat16)
    return (grad_queries, grad_keys, grad_values)


def solution(mesh):
    return jax.shard_map(
        shards,
        mesh=mesh,
        in_specs=(
            P(("groups", "head", "blk"), None),
            P(("groups", "head", "blk"), None),
            P(("groups", "head", "blk"), None),
            P(("groups", "head", "blk"), None),
            P(("groups", "head", "blk"), None),
            P(("groups", "head", "blk"), None),
            P("groups", None),
            P("groups"),
        ),
        out_specs=(
            P(("groups", "head", "blk"), None),
            P(("groups", "head", "blk"), None),
            P(("groups", "head", "blk"), None),
        ),
        check_vma=False,
    )
```

profile of v0, /device:TPU:0, one launch (start us, length us, event | category | flops | bytes accessed | tf_op | source)
XLA Modules:
  0.0 115.2 jit_solution(6683661105864896199)
XLA Ops:
  0.6 1.0 convert_bitcast_fusion
  1.7 0.8 copy-done.1
  2.8 13.7 %all_to_all.143 = f32[32,8,2]{0,2,1:T(2,128)S(1)} all-to-all(f32[32,8,2]{0,2,1:T(2,128)S(1)} %bitcast.160), channel_id=1, replica_groups=mesh['groups'=2,'head'=8,'blk'=2] {'head'}, dimensions={1} | all-to-all | bytes 4096 | tf_op jit(solution)/shard_map/all_to_all | solution.py:91
  16.4 3.3 %all-to-all-start.3 = ((f32[32,8,2]{0,2,1:T(2,128)}), f32[32,8,2]{0,2,1:T(2,128)S(1)}, u32[]{:S(2)}, u32[]{:S(2)}) async-start(f32[32,8,2]{0,2,1:T(2,128)} %bitcast.13), calls=%async_computation.3 | async-start | bytes 16384 | tf_op jit(solution)/shard_map/all_to_all | solution.py:90
  19.8 6.4 %all-to-all-done.3 = f32[32,8,2]{0,2,1:T(2,128)S(1)} async-done(((f32[32,8,2]{0,2,1:T(2,128)}), f32[32,8,2]{0,2,1:T(2,128)S(1)}, u32[]{:S(2)}, u32[]{:S(2)}) %all-to-all-start.3) | async-done | bytes 2080 | tf_op jit(solution)/shard_map/all_to_all | solution.py:90
  26.2 0.7 broadcast_in_dim.88
  26.9 3.5 %all-to-all-start = ((bf16[32,16,128]{2,0,1:T(8,128)(2,1)}), bf16[32,16,128]{2,0,1:T(8,128)(2,1)S(1)}, u32[]{:S(2)}, u32[]{:S(2)}) async-start(bf16[32,16,128]{2,0,1:T(8,128)(2,1)} %bitcast), calls=%async_computation | async-start | bytes 262144 | tf_op jit(solution)/shard_map/all_to_all | solution.py:86
  30.5 7.3 %all-to-all-done = bf16[32,16,128]{2,0,1:T(8,128)(2,1)S(1)} async-done(((bf16[32,16,128]{2,0,1:T(8,128)(2,1)}), bf16[32,16,128]{2,0,1:T(8,128)(2,1)S(1)}, u32[]{:S(2)}, u32[]{:S(2)}) %all-to-all-start) | async-done | bytes 131104 | tf_op jit(solution)/shard_map/all_to_all | solution.py:86
  37.7 0.7 broadcast_in_dim.89
  38.4 3.4 %all-to-all-start.1 = ((bf16[32,16,128]{2,0,1:T(8,128)(2,1)}), bf16[32,16,128]{2,0,1:T(8,128)(2,1)S(1)}, u32[]{:S(2)}, u32[]{:S(2)}) async-start(bf16[32,16,128]{2,0,1:T(8,128)(2,1)} %bitcast.4), calls=%async_computation.1 | async-start | bytes 262144 | tf_op jit(solution)/shard_map/all_to_all | solution.py:87
  41.8 0.7 copy_bitcast_fusion.1
  42.5 6.6 %all-to-all-done.1 = bf16[32,16,128]{2,0,1:T(8,128)(2,1)S(1)} async-done(((bf16[32,16,128]{2,0,1:T(8,128)(2,1)}), bf16[32,16,128]{2,0,1:T(8,128)(2,1)S(1)}, u32[]{:S(2)}, u32[]{:S(2)}) %all-to-all-start.1) | async-done | bytes 131104 | tf_op jit(solution)/shard_map/all_to_all | solution.py:87
  49.0 3.4 %all-to-all-start.2 = ((bf16[32,16,128]{2,0,1:T(8,128)(2,1)}), bf16[32,16,128]{2,0,1:T(8,128)(2,1)S(1)}, u32[]{:S(2)}, u32[]{:S(2)}) async-start(bf16[32,16,128]{2,0,1:T(8,128)(2,1)} %copy_bitcast_fusion.1), calls=%async_computation.2 | async-start | bytes 262144 | tf_op jit(solution)/shard_map/all_to_all | solution.py:84
  52.4 0.7 copy_bitcast_fusion
  53.1 6.6 %all-to-all-done.2 = bf16[32,16,128]{2,0,1:T(8,128)(2,1)S(1)} async-done(((bf16[32,16,128]{2,0,1:T(8,128)(2,1)}), bf16[32,16,128]{2,0,1:T(8,128)(2,1)S(1)}, u32[]{:S(2)}, u32[]{:S(2)}) %all-to-all-start.2) | async-done | bytes 131104 | tf_op jit(solution)/shard_map/all_to_all | solution.py:84
  59.7 3.5 %all-to-all-start.4 = ((bf16[32,16,128]{2,0,1:T(8,128)(2,1)}), bf16[32,16,128]{2,0,1:T(8,128)(2,1)S(1)}, u32[]{:S(2)}, u32[]{:S(2)}) async-start(bf16[32,16,128]{2,0,1:T(8,128)(2,1)} %copy_bitcast_fusion), calls=%async_computation.4 | async-start | bytes 262144 | tf_op jit(solution)/shard_map/all_to_all | solution.py:85
  63.4 0.5 copy-done.4
  64.4 6.1 %all-to-all-done.4 = bf16[32,16,128]{2,0,1:T(8,128)(2,1)S(1)} async-done(((bf16[32,16,128]{2,0,1:T(8,128)(2,1)}), bf16[32,16,128]{2,0,1:T(8,128)(2,1)S(1)}, u32[]{:S(2)}, u32[]{:S(2)}) %all-to-all-start.4) | async-done | bytes 131104 | tf_op jit(solution)/shard_map/all_to_all | solution.py:85
  70.6 8.2 %while.29 = (s32[]{:T(128)}, bf16[256,2,128]{2,0,1:T(8,128)(2,1)S(1)}, bf16[256,2,128]{2,0,1:T(8,128)(2,1)S(1)}, f32[256,2,128]{2,0,1:T(8,128)S(1)}, f32[256,2,1...) while((s32[]{:T(128)}, ...), condition=%wide.region_5.6_spmd.clone.clone.clone, body=%wide.region_2.5_spmd.clone.clone.clone.sunk | while | flops 172717072 | bytes 8807412 | solution.py:116
  70.8 0.3 fusion.81
  71.3 0.3 fusion.82
  71.8 0.3 fusion.84
  72.2 0.3 fusion.85
  72.5 0.6 collective-permute-start.3
  73.1 0.4 collective-permute-start.1
  73.6 0.3 fusion.86
  73.8 0.6 collective-permute-done
  74.8 0.3 fusion.81
  75.3 0.3 fusion.82
  75.8 0.3 fusion.84
  76.1 0.4 collective-permute-start.2
  76.5 0.3 fusion.85
  77.0 0.4 collective-permute-start
  77.5 0.3 fusion.86
  77.8 0.8 collective-permute-done
  78.8 0.9 copy.127
  79.7 3.4 %all-to-all-start.6 = ((bf16[256,2,128]{2,1,0:T(2,128)(2,1)}), bf16[256,2,128]{2,1,0:T(2,128)(2,1)S(1)}, u32[]{:S(2)}, u32[]{:S(2)}) async-start(bf16[256,2,128]{2,1,0:T(2,128)(2,1)} %copy.127), calls=%async_computation.6 | async-start | bytes 262144 | tf_op jit(solution)/shard_map/all_to_all | solution.py:118
  83.1 0.9 copy.106
  83.9 6.6 %all-to-all-done.6 = bf16[256,2,128]{2,1,0:T(2,128)(2,1)S(1)} async-done(((bf16[256,2,128]{2,1,0:T(2,128)(2,1)}), bf16[256,2,128]{2,1,0:T(2,128)(2,1)S(1)}, u32[]{:S(2)}, u32[]{:S(2)}) %all-to-all-start.6) | async-done | bytes 131104 | tf_op jit(solution)/shard_map/all_to_all | solution.py:118
  90.6 3.4 %all-to-all-start.7 = ((f32[256,2,128]{2,1,0:T(2,128)}), f32[256,2,128]{2,1,0:T(2,128)S(1)}, u32[]{:S(2)}, u32[]{:S(2)}) async-start(f32[256,2,128]{2,1,0:T(2,128)} %copy.106), calls=%async_computation.7 | async-start | bytes 524288 | tf_op jit(solution)/shard_map/all_to_all | solution.py:123
  94.0 0.9 copy.108
  94.9 7.4 %all-to-all-done.7 = f32[256,2,128]{2,1,0:T(2,128)S(1)} async-done(((f32[256,2,128]{2,1,0:T(2,128)}), f32[256,2,128]{2,1,0:T(2,128)S(1)}, u32[]{:S(2)}, u32[]{:S(2)}) %all-to-all-start.7) | async-done | bytes 262176 | tf_op jit(solution)/shard_map/all_to_all | solution.py:123
  102.3 3.4 %all-to-all-start.8 = ((f32[256,2,128]{2,1,0:T(2,128)}), f32[256,2,128]{2,1,0:T(2,128)S(1)}, u32[]{:S(2)}, u32[]{:S(2)}) async-start(f32[256,2,128]{2,1,0:T(2,128)} %copy.108), calls=%async_computation.8 | async-start | bytes 524288 | tf_op jit(solution)/shard_map/all_to_all | solution.py:124
  105.8 0.7 reshape.258
  106.5 0.3 reduce_sum.88
  106.8 7.4 %all-to-all-done.8 = f32[256,2,128]{2,1,0:T(2,128)S(1)} async-done(((f32[256,2,128]{2,1,0:T(2,128)}), f32[256,2,128]{2,1,0:T(2,128)S(1)}, u32[]{:S(2)}, u32[]{:S(2)}) %all-to-all-start.8) | async-done | bytes 262176 | tf_op jit(solution)/shard_map/all_to_all | solution.py:124
  114.2 0.3 reduce_sum.93
  114.5 0.6 copy_bitcast_fusion.2
  (61 shorter events, 3.2 us)
Async XLA Ops:
  0.6 41.1 %copy-start = (bf16[32,2048]{1,0:T(8,128)(2,1)S(1)}, bf16[32,2048]{1,0:T(8,128)(2,1)}, u32[]{:S(2)}) copy-start(bf16[32,2048]{1,0:T(8,128)(2,1)} %param.10) | copy-start | bytes 393220
  1.6 0.9 copy-start.1
  2.8 17.0 %copy-start.2 = (bf16[32,256]{1,0:T(8,128)(2,1)S(1)}, bf16[32,256]{1,0:T(8,128)(2,1)}, u32[]{:S(2)}) copy-start(bf16[32,256]{1,0:T(8,128)(2,1)} %param.11) | copy-start | bytes 49156
  16.4 9.8 %all-to-all-start.3 = ((f32[32,8,2]{0,2,1:T(2,128)}), f32[32,8,2]{0,2,1:T(2,128)S(1)}, u32[]{:S(2)}, u32[]{:S(2)}) async-start(f32[32,8,2]{0,2,1:T(2,128)} %bitcast.13), calls=%async_computation.3 | async-start | bytes 16384 | tf_op jit(solution)/shard_map/all_to_all | solution.py:90
  26.9 3.5 %copy-start.3 = (bf16[32,256]{1,0:T(8,128)(2,1)S(1)}, bf16[32,256]{1,0:T(8,128)(2,1)}, u32[]{:S(2)}) copy-start(bf16[32,256]{1,0:T(8,128)(2,1)} %param.12) | copy-start | bytes 49156
  26.9 10.8 %all-to-all-start = ((bf16[32,16,128]{2,0,1:T(8,128)(2,1)}), bf16[32,16,128]{2,0,1:T(8,128)(2,1)S(1)}, u32[]{:S(2)}, u32[]{:S(2)}) async-start(bf16[32,16,128]{2,0,1:T(8,128)(2,1)} %bitcast), calls=%async_computation | async-start | bytes 262144 | tf_op jit(solution)/shard_map/all_to_all | solution.py:86
  38.4 10.7 %all-to-all-start.1 = ((bf16[32,16,128]{2,0,1:T(8,128)(2,1)}), bf16[32,16,128]{2,0,1:T(8,128)(2,1)S(1)}, u32[]{:S(2)}, u32[]{:S(2)}) async-start(bf16[32,16,128]{2,0,1:T(8,128)(2,1)} %bitcast.4), calls=%async_computation.1 | async-start | bytes 262144 | tf_op jit(solution)/shard_map/all_to_all | solution.py:87
  49.0 10.7 %all-to-all-start.2 = ((bf16[32,16,128]{2,0,1:T(8,128)(2,1)}), bf16[32,16,128]{2,0,1:T(8,128)(2,1)S(1)}, u32[]{:S(2)}, u32[]{:S(2)}) async-start(bf16[32,16,128]{2,0,1:T(8,128)(2,1)} %copy_bitcast_fusion.1), calls=%async_computation.2 | async-start | bytes 262144 | tf_op jit(solution)/shard_map/all_to_all | solution.py:84
  59.7 3.6 %copy-start.5 = (s32[4]{0:T(128)S(1)}, s32[4]{0:T(128)}, u32[]{:S(2)}) copy-start(s32[4]{0:T(128)} %param.17) | copy-start | bytes 52
  59.7 10.8 %all-to-all-start.4 = ((bf16[32,16,128]{2,0,1:T(8,128)(2,1)}), bf16[32,16,128]{2,0,1:T(8,128)(2,1)S(1)}, u32[]{:S(2)}, u32[]{:S(2)}) async-start(bf16[32,16,128]{2,0,1:T(8,128)(2,1)} %copy_bitcast_fusion), calls=%async_computation.4 | async-start | bytes 262144 | tf_op jit(solution)/shard_map/all_to_all | solution.py:85
  63.2 0.7 copy-start.4
  72.1 2.5 %collective-permute-start.2 = (f32[256,2,128]{2,0,1:T(8,128)S(1)}, f32[256,2,128]{2,0,1:T(8,128)S(1)}, u32[]{:S(2)}, u32[]{:S(2)}) collective-permute-start(f32[256,2,128]{2,0,1:T(8,128)S(1)} %fusion.84), channel_id=1, source_target_pairs={{0,1},{1,0},{2,3},{3,2},{4,5},{5,4},{6,7},{7,6},{8,9},{9,8},{10,11... | collective-permute-start | bytes 786440 | tf_op jit(solution)/shard_map/while/body/eval_jaxpr/ppermute | solution.py:17
  72.5 2.1 %collective-permute-start.3 = (f32[256,2,128]{2,0,1:T(8,128)S(1)}, f32[256,2,128]{2,0,1:T(8,128)S(1)}, u32[]{:S(2)}, u32[]{:S(2)}) collective-permute-start(f32[256,2,128]{2,0,1:T(8,128)S(1)} %fusion.85), channel_id=1, source_target_pairs={{0,1},{1,0},{2,3},{3,2},{4,5},{5,4},{6,7},{7,6},{8,9},{9,8},{10,11... | collective-permute-start | bytes 786440 | tf_op jit(solution)/shard_map/while/body/eval_jaxpr/ppermute | solution.py:17
  73.0 1.3 %collective-permute-start = (bf16[256,2,128]{2,0,1:T(8,128)(2,1)S(1)}, bf16[256,2,128]{2,0,1:T(8,128)(2,1)S(1)}, u32[]{:S(2)}, u32[]{:S(2)}) collective-permute-start(bf16[256,2,128]{2,0,1:T(8,128)(2,1)S(1)} %copy.137), channel_id=1, source_target_pairs={{0,1},{1,0},{2,3},{3,2},{4,5},{5,4},{6,7},{7,6},{8,9},{9,8},{10,11... | collective-permute-start | bytes 393224 | tf_op jit(solution)/shard_map/while/body/eval_jaxpr/ppermute | solution.py:17
  73.1 1.5 %collective-permute-start.1 = (bf16[256,2,128]{2,0,1:T(8,128)(2,1)S(1)}, bf16[256,2,128]{2,0,1:T(8,128)(2,1)S(1)}, u32[]{:S(2)}, u32[]{:S(2)}) collective-permute-start(bf16[256,2,128]{2,0,1:T(8,128)(2,1)S(1)} %copy.138), channel_id=1, source_target_pairs={{0,1},{1,0},{2,3},{3,2},{4,5},{5,4},{6,7},{7,6},{8,9},{9,8},{10,11... | collective-permute-start | bytes 393224 | tf_op jit(solution)/shard_map/while/body/eval_jaxpr/ppermute | solution.py:17
  76.1 2.7 %collective-permute-start.2 = (f32[256,2,128]{2,0,1:T(8,128)S(1)}, f32[256,2,128]{2,0,1:T(8,128)S(1)}, u32[]{:S(2)}, u32[]{:S(2)}) collective-permute-start(f32[256,2,128]{2,0,1:T(8,128)S(1)} %fusion.84), channel_id=1, source_target_pairs={{0,1},{1,0},{2,3},{3,2},{4,5},{5,4},{6,7},{7,6},{8,9},{9,8},{10,11... | collective-permute-start | bytes 786440 | tf_op jit(solution)/shard_map/while/body/eval_jaxpr/ppermute | solution.py:17
  76.8 2.0 %collective-permute-start.3 = (f32[256,2,128]{2,0,1:T(8,128)S(1)}, f32[256,2,128]{2,0,1:T(8,128)S(1)}, u32[]{:S(2)}, u32[]{:S(2)}) collective-permute-start(f32[256,2,128]{2,0,1:T(8,128)S(1)} %fusion.85), channel_id=1, source_target_pairs={{0,1},{1,0},{2,3},{3,2},{4,5},{5,4},{6,7},{7,6},{8,9},{9,8},{10,11... | collective-permute-start | bytes 786440 | tf_op jit(solution)/shard_map/while/body/eval_jaxpr/ppermute | solution.py:17
  77.0 1.6 %collective-permute-start = (bf16[256,2,128]{2,0,1:T(8,128)(2,1)S(1)}, bf16[256,2,128]{2,0,1:T(8,128)(2,1)S(1)}, u32[]{:S(2)}, u32[]{:S(2)}) collective-permute-start(bf16[256,2,128]{2,0,1:T(8,128)(2,1)S(1)} %copy.137), channel_id=1, source_target_pairs={{0,1},{1,0},{2,3},{3,2},{4,5},{5,4},{6,7},{7,6},{8,9},{9,8},{10,11... | collective-permute-start | bytes 393224 | tf_op jit(solution)/shard_map/while/body/eval_jaxpr/ppermute | solution.py:17
  77.4 1.4 %collective-permute-start.1 = (bf16[256,2,128]{2,0,1:T(8,128)(2,1)S(1)}, bf16[256,2,128]{2,0,1:T(8,128)(2,1)S(1)}, u32[]{:S(2)}, u32[]{:S(2)}) collective-permute-start(bf16[256,2,128]{2,0,1:T(8,128)(2,1)S(1)} %copy.138), channel_id=1, source_target_pairs={{0,1},{1,0},{2,3},{3,2},{4,5},{5,4},{6,7},{7,6},{8,9},{9,8},{10,11... | collective-permute-start | bytes 393224 | tf_op jit(solution)/shard_map/while/body/eval_jaxpr/ppermute | solution.py:17
  79.7 10.9 %all-to-all-start.6 = ((bf16[256,2,128]{2,1,0:T(2,128)(2,1)}), bf16[256,2,128]{2,1,0:T(2,128)(2,1)S(1)}, u32[]{:S(2)}, u32[]{:S(2)}) async-start(bf16[256,2,128]{2,1,0:T(2,128)(2,1)} %copy.127), calls=%async_computation.6 | async-start | bytes 262144 | tf_op jit(solution)/shard_map/all_to_all | solution.py:118
  90.6 11.7 %all-to-all-start.7 = ((f32[256,2,128]{2,1,0:T(2,128)}), f32[256,2,128]{2,1,0:T(2,128)S(1)}, u32[]{:S(2)}, u32[]{:S(2)}) async-start(f32[256,2,128]{2,1,0:T(2,128)} %copy.106), calls=%async_computation.7 | async-start | bytes 524288 | tf_op jit(solution)/shard_map/all_to_all | solution.py:123
  102.3 11.9 %all-to-all-start.8 = ((f32[256,2,128]{2,1,0:T(2,128)}), f32[256,2,128]{2,1,0:T(2,128)S(1)}, u32[]{:S(2)}, u32[]{:S(2)}) async-start(f32[256,2,128]{2,1,0:T(2,128)} %copy.108), calls=%async_computation.8 | async-start | bytes 524288 | tf_op jit(solution)/shard_map/all_to_all | solution.py:124
where the time goes:
time: 116 us; the launch traced here: 115 us
  waiting for transfers between devices  56.1 us (48%)
  starting transfers between devices  29.6 us (26%)
  blocking collectives  13.7 us (12%)
  local copies, waits for them, and re-layouts  8.98 us (8%)
  matrix products  3.54 us (3%)
  other arithmetic  2.25 us (2%)
    all_to_all x1, blocking collectives, shards(): lax.all_to_all(row_delta, 'head', split_axis=1, concat_axis=0, tiled=True)  13.7 us
    all_to_all x1, waiting for transfers between devices, shards(): lax.all_to_all(key_grad, 'head', split_axis=0, concat_axis=1, tiled=True)  7.38 us
    all_to_all x1, waiting for transfers between devices, shards(): lax.all_to_all(value_grad, 'head', split_axis=0, concat_axis=1, tiled=True)  7.37 us
    all_to_all x1, waiting for transfers between devices, shards(): lax.all_to_all(key_heads, 'head', split_axis=1, concat_axis=0, tiled=True)  7.25 us
    all_to_all x1, waiting for transfers between devices, shards(): lax.all_to_all(query_grad.astype(jnp.bfloat16), 'head', split_axis=0, con...  6.61 us
    all_to_all x1, waiting for transfers between devices, shards(): lax.all_to_all(query_heads, 'head', split_axis=1, concat_axis=0, tiled=True)  6.6 us
    all_to_all x1, waiting for transfers between devices, shards(): lax.all_to_all(value_heads, 'head', split_axis=1, concat_axis=0, tiled=True)  6.59 us
    all_to_all x1, waiting for transfers between devices, shards(): lax.all_to_all(log_norm, 'head', split_axis=1, concat_axis=0, tiled=True)  6.43 us
  transfers between devices with their start and end apart: 16, of which 12 were waited for; matrix products, arithmetic and copies ran while one was open for 5% of the time, Pallas kernels for 0%

commit v1 on v0

v1 whole, which is shorter than its diff:
```python
import functools
import math

import jax
import jax.numpy as jnp
from jax import lax
from jax.experimental import pallas as pl
from jax.experimental.pallas import tpu as pltpu
from jax.sharding import PartitionSpec as P

BLOCK = 128
CORES = 2
MESH = pl.DeviceIdType.MESH
NT = (((1,), (1,)), ((), ()))
TN = (((0,), (0,)), ((), ()))
NN = (((1,), (0,)), ((), ()))


def dot(a, b, dims):
    return lax.dot_general(a, b, dims, preferred_element_type=jnp.float32)


def each(first, last, body):
    if last - first <= 8:
        for k in range(first, last):
            body(k)
    else:
        lax.fori_loop(first, last, lambda k, c: (body(k), c)[1], 0)


def kernel(
    chips, reach, blk_size, group,
    vis_ref, seg_ref, q_hbm, k_hbm, v_hbm, o_hbm, g_hbm, l_hbm,
    dq_ref, dk_ref, dv_ref,
    q_in, k_in, v_in, o_in, g_in, l_in, in_sem,
    rows, rows_out, kv_out, kv, ds_all, part, back, own_part, dq_out, dq_back,
    x_send, x_recv, kv_send, kv_recv, part_send, part_recv, dq_send, dq_recv,
):
    tok, width = q_in.shape
    dh = k_in.shape[1] // CORES
    half = group * dh
    scale = 1.0 / math.sqrt(dh)
    spot = lax.axis_index("head") * blk_size + lax.axis_index("blk")
    chip, core = spot // CORES, spot % CORES
    other = 1 - core

    def at(its_chip, its_core):
        where = its_chip * CORES + its_core
        return {"head": where // blk_size, "blk": where % blk_size}

    def on_chips(first, last, sign, body):
        def one(k):
            its_chip = chip + sign * k

            @pl.when((its_chip >= 0) & (its_chip < chips))
            def _():
                body(k, its_chip)

        each(first, last, one)

    barrier = pltpu.get_barrier_semaphore()

    def greet(k, its_chip):
        for c in range(CORES):
            pl.semaphore_signal(barrier, inc=1, device_id=at(its_chip, c), device_id_type=MESH)

    loads = [
        pltpu.make_async_copy(src, dst, in_sem.at[i])
        for i, (src, dst) in enumerate(
            ((k_hbm, k_in), (v_hbm, v_in), (q_hbm, q_in), (g_hbm, g_in), (o_hbm, o_in), (l_hbm, l_in))
        )
    ]
    for load in loads:
        load.start()
    pl.semaphore_signal(barrier, inc=1, device_id=at(chip, other), device_id_type=MESH)
    on_chips(1, reach + 1, 1, greet)
    on_chips(1, reach + 1, -1, greet)

    loads[0].wait()
    loads[1].wait()
    for c in range(CORES):
        kv_out[c, 0] = k_in[:, c * dh : (c + 1) * dh]
        kv_out[c, 1] = v_in[:, c * dh : (c + 1) * dh]
    kv[0, pl.ds(core, 1)] = kv_out[pl.ds(core, 1)]

    near = jnp.minimum(chip, reach) + jnp.minimum(chips - 1 - chip, reach)
    pl.semaphore_wait(barrier, CORES * near + 1)

    def kv_copy(k, its_chip, its_core):
        return pltpu.make_async_remote_copy(
            src_ref=kv_out.at[its_core],
            dst_ref=kv.at[k, core],
            send_sem=kv_send.at[k, its_core],
            recv_sem=kv_recv.at[k, core],
            device_id=at(its_chip, its_core),
            device_id_type=MESH,
        )

    def kv_arrived(k, its_chip, its_core):
        pltpu.make_async_remote_copy(
            src_ref=kv_out.at[0],
            dst_ref=kv.at[k, its_core],
            send_sem=kv_send.at[k, its_core],
            recv_sem=kv_recv.at[k, its_core],
            device_id=at(its_chip, its_core),
            device_id_type=MESH,
        ).wait_recv()

    def send_kv(k, its_chip):
        for c in range(CORES):
            kv_copy(k, its_chip, c).start()

    on_chips(1, reach + 1, 1, send_kv)
    kv_copy(0, chip, other).start()

    for load in loads[2:]:
        load.wait()

    lane = lax.broadcasted_iota(jnp.int32, (tok, dh), 1)

    def prepare(h, column):
        at_h = pl.ds(pl.multiple_of(column * dh, dh), dh)
        g_h = g_in[:, at_h]
        delta = jnp.sum(g_h.astype(jnp.float32) * o_in[:, at_h].astype(jnp.float32), axis=1, keepdims=True)
        return at_h, g_h, delta

    def extra(lse, delta):
        value = jnp.where(lane < 3, lse * (1.0 / scale), jnp.where(lane < 6, delta, 0.0))
        high = value.astype(jnp.bfloat16).astype(jnp.float32)
        rest = value - high
        middle = rest.astype(jnp.bfloat16).astype(jnp.float32)
        third = (lane == 0) | (lane == 3)
        second = (lane == 1) | (lane == 4)
        return jnp.where(third, high, jnp.where(second, middle, rest - middle)).astype(jnp.bfloat16)

    def fill(target, mine):
        base = mine * group
        lse_all = jnp.where(mine == 0, l_in[:, :group], l_in[:, group:])
        for h in range(group):
            at_h, g_h, delta = prepare(h, base + h)
            r = slice(h * tok, (h + 1) * tok)
            target[0, r] = q_in[:, at_h]
            target[1, r] = extra(lse_all[:, h : h + 1], delta)
            target[2, r] = g_h

    fill(rows_out, other)
    x_copy = pltpu.make_async_remote_copy(
        src_ref=rows_out,
        dst_ref=rows.at[core],
        send_sem=x_send,
        recv_sem=x_recv,
        device_id=at(chip, other),
        device_id_type=MESH,
    )
    x_copy.start()
    fill(rows.at[core], core)

    n_rows = group * tok
    row_iota = lax.broadcasted_iota(jnp.int32, (1, n_rows), 1) % tok
    starts, spots = [], []
    for e in range(CORES):
        query_pos = (chip * CORES + e) * tok + row_iota
        start = jnp.zeros_like(query_pos)
        end = jnp.int32(0)
        for s in range(seg_ref.shape[0]):
            end = end + seg_ref[s]
            start = jnp.where(query_pos >= end, end, start)
        starts.append(start)
        spots.append(query_pos)
    chunk = CORES * tok
    chunk_lane = lax.broadcasted_iota(jnp.int32, (chunk, dh), 1)
    minus_lse = jnp.where(chunk_lane < 3, -1.0, 0.0).astype(jnp.bfloat16)
    minus_delta = jnp.where((chunk_lane >= 3) & (chunk_lane < 6), -1.0, 0.0).astype(jnp.bfloat16)
    key_iota = lax.broadcasted_iota(jnp.int32, (chunk, n_rows), 0)
    my_block = chip * chunk // BLOCK
    far = chips * chunk

    def grads(k, its_chip, diagonal):
        keys = jnp.concatenate([kv[k, 0, 0], kv[k, 1, 0]], axis=0)
        values = jnp.concatenate([kv[k, 0, 1], kv[k, 1, 1]], axis=0)
        keys_more = jnp.concatenate([keys, minus_lse], axis=1)
        values_more = jnp.concatenate([values, minus_delta], axis=1)
        seen = vis_ref[my_block, its_chip * chunk // BLOCK]
        key_pos = key_iota + its_chip * chunk
        key_grad = value_grad = None
        for e in range(CORES):
            q, more, g = rows[e, 0], rows[e, 1], rows[e, 2]
            scores = dot(keys_more, jnp.concatenate([q, more], axis=1), NT)
            grad_prob = dot(values_more, jnp.concatenate([g, more], axis=1), NT)
            allowed = key_pos >= jnp.where(seen > 0, starts[e], far)
            if diagonal:
                allowed = allowed & (key_pos <= spots[e])
            prob = jnp.where(allowed, jnp.exp(scores * scale), 0.0)
            grad_score = (prob * grad_prob * scale).astype(jnp.bfloat16)
            v_part = dot(prob.astype(jnp.bfloat16), g, NN)
            k_part = dot(grad_score, q, NN)
            ds_all[k, :, e * n_rows : (e + 1) * n_rows] = grad_score
            key_grad = k_part if key_grad is None else key_grad + k_part
            value_grad = v_part if value_grad is None else value_grad + v_part
        for e in range(CORES):
            part[k, e, 0] = key_grad[e * tok : (e + 1) * tok].astype(jnp.bfloat16)
            part[k, e, 1] = value_grad[e * tok : (e + 1) * tok].astype(jnp.bfloat16)
        return key_grad, value_grad

    def part_copy(k, its_chip, its_core):
        return pltpu.make_async_remote_copy(
            src_ref=part.at[k, its_core],
            dst_ref=back.at[k, core],
            send_sem=part_send.at[k, its_core],
            recv_sem=part_recv.at[k, core],
            device_id=at(its_chip, its_core),
            device_id_type=MESH,
        )

    def part_arrived(k, its_chip, its_core):
        pltpu.make_async_remote_copy(
            src_ref=part.at[k, its_core],
            dst_ref=back.at[k, its_core],
            send_sem=part_send.at[k, its_core],
            recv_sem=part_recv.at[k, its_core],
            device_id=at(its_chip, its_core),
            device_id_type=MESH,
        ).wait_recv()

    kv_arrived(0, chip, other)
    x_copy.wait_recv()
    grads(0, chip, True)
    part_copy(0, chip, other).start()
    back[0, pl.ds(core, 1)] = part[0, pl.ds(core, 1)]

    def one_chunk(k):
        its_chip = chip - k

        @pl.when(its_chip >= 0)
        def _():
            for e in range(CORES):
                kv_arrived(k, its_chip, e)
            grads(k, its_chip, False)
            for e in range(CORES):
                part_copy(k, its_chip, e).start()

        @pl.when(its_chip < 0)
        def _():
            kv[k] = jnp.zeros(kv.shape[1:], kv.dtype)
            ds_all[k] = jnp.zeros(ds_all.shape[1:], ds_all.dtype)

    each(1, reach + 1, one_chunk)

    total = reach + 1
    at_once = max(n for n in range(1, 9) if total % n == 0)

    def query_part(first):
        scores = jnp.concatenate([ds_all[first + i] for i in range(at_once)], axis=0)
        keys = jnp.concatenate(
            [kv[first + i, e, 0] for i in range(at_once) for e in range(CORES)], axis=0
        )
        return dot(scores, keys, TN)

    if total == at_once:
        query_grad = query_part(0)
    else:
        query_grad = lax.fori_loop(
            0, total // at_once, lambda i, acc: acc + query_part(i * at_once),
            jnp.zeros((CORES * n_rows, dh), jnp.float32),
        )
    for e in range(CORES):
        dq_out[e] = query_grad[e * n_rows : (e + 1) * n_rows].astype(jnp.bfloat16)
    dq_copy = pltpu.make_async_remote_copy(
        src_ref=dq_out.at[other],
        dst_ref=dq_back,
        send_sem=dq_send,
        recv_sem=dq_recv,
        device_id=at(chip, other),
        device_id_type=MESH,
    )
    dq_copy.start()
    for h in range(group):
        r = slice(h * tok, (h + 1) * tok)
        dq_ref[:, pl.ds(pl.multiple_of((core * group + h) * dh, dh), dh)] = dq_out[core, r]
    dq_copy.wait_recv()
    for h in range(group):
        r = slice(h * tok, (h + 1) * tok)
        dq_ref[:, pl.ds(pl.multiple_of((other * group + h) * dh, dh), dh)] = dq_back[r]

    part_arrived(0, chip, other)
    for c in range(CORES):
        for which in range(2):
            own_part[c, which] = back[0, c, which].astype(jnp.float32)

    def add(k, its_chip):
        for c in range(CORES):
            part_arrived(k, its_chip, c)
            own_part[c] += back[k, c].astype(jnp.float32)

    on_chips(1, reach + 1, 1, add)
    for c in range(CORES):
        dk_ref[:, c * dh : (c + 1) * dh] = own_part[c, 0].astype(jnp.bfloat16)
        dv_ref[:, c * dh : (c + 1) * dh] = own_part[c, 1].astype(jnp.bfloat16)

    x_copy.wait_send()
    dq_copy.wait_send()
    kv_copy(0, chip, other).wait_send()
    part_copy(0, chip, other).wait_send()

    def kv_left(k, its_chip):
        for c in range(CORES):
            kv_copy(k, its_chip, c).wait_send()

    def part_left(k, its_chip):
        for c in range(CORES):
            part_copy(k, its_chip, c).wait_send()

    on_chips(1, reach + 1, 1, kv_left)
    on_chips(1, reach + 1, -1, part_left)


def solution(mesh):
    blk_size = mesh.shape["blk"]
    devices = mesh.shape["head"] * blk_size
    chips = devices // CORES

    def shards(queries, key_rows, value_rows, fwd_output, grad_out, log_norm, visible, seg_lengths):
        tok, width = queries.shape
        heads = log_norm.shape[1]
        dh = width // heads
        kv_heads = key_rows.shape[1] // dh
        assert kv_heads == CORES and blk_size % CORES == 0 and BLOCK % (CORES * tok) == 0
        group = heads // kv_heads
        longest = devices * tok // 2
        reach = min(pl.cdiv(longest - 1, CORES * tok), chips - 1)
        n_rows = group * tok
        bf16, f32 = jnp.bfloat16, jnp.float32
        slots = reach + 1
        dma = pltpu.SemaphoreType.DMA
        return pl.pallas_call(
            functools.partial(kernel, chips, reach, blk_size, group),
            out_shape=(
                jax.ShapeDtypeStruct(queries.shape, bf16),
                jax.ShapeDtypeStruct(key_rows.shape, bf16),
                jax.ShapeDtypeStruct(value_rows.shape, bf16),
            ),
            in_specs=[pl.BlockSpec(memory_space=pltpu.SMEM)] * 2
            + [pl.BlockSpec(memory_space=pl.ANY)] * 6,
            out_specs=[pl.BlockSpec(memory_space=pltpu.VMEM)] * 3,
            scratch_shapes=[
                pltpu.VMEM(queries.shape, bf16),
                pltpu.VMEM(key_rows.shape, bf16),
                pltpu.VMEM(value_rows.shape, bf16),
                pltpu.VMEM(fwd_output.shape, bf16),
                pltpu.VMEM(grad_out.shape, bf16),
                pltpu.VMEM(log_norm.shape, f32),
                dma((6,)),
                pltpu.VMEM((CORES, 3, n_rows, dh), bf16),
                pltpu.VMEM((3, n_rows, dh), bf16),
                pltpu.VMEM((CORES, 2, tok, dh), bf16),
                pltpu.VMEM((slots, CORES, 2, tok, dh), bf16),
                pltpu.VMEM((slots, CORES * tok, CORES * n_rows), bf16),
                pltpu.VMEM((slots, CORES, 2, tok, dh), bf16),
                pltpu.VMEM((slots, CORES, 2, tok, dh), bf16),
                pltpu.VMEM((CORES, 2, tok, dh), f32),
                pltpu.VMEM((CORES, n_rows, dh), bf16),
                pltpu.VMEM((n_rows, dh), bf16),
                dma, dma,
                dma((slots, CORES)), dma((slots, CORES)),
                dma((slots, CORES)), dma((slots, CORES)),
                dma, dma,
            ],
            compiler_params=pltpu.CompilerParams(
                collective_id=0, has_side_effects=True, vmem_limit_bytes=48 << 20
            ),
        )(visible, seg_lengths, queries, key_rows, value_rows, fwd_output, grad_out, log_norm)

    tokens = P(("groups", "head", "blk"), None)
    return jax.shard_map(
        shards,
        mesh=mesh,
        in_specs=(tokens,) * 6 + (P("groups", None), P("groups")),
        out_specs=(tokens,) * 3,
        check_vma=False,
    )
```

time: 116 us -> 23.2 us (0.20)
  waiting for transfers between devices: 56.1 us -> 0 us
  starting transfers between devices: 29.6 us -> 0 us
  Pallas kernels: 0 us -> 16.1 us
  blocking collectives: 13.7 us -> 0 us
  matrix products: 3.54 us -> 0 us
  local copies, waits for them, and re-layouts: 8.98 us -> 6.09 us
  other arithmetic: 2.25 us -> 0 us
    all_to_all x8 -> x0, waiting for transfers between devices: 54.3 us -> none  [the longest x1 7.38 us: shards(): lax.all_to_all(key_grad, 'head', split_axis=0, concat_axis=1, tiled=True)]
    all_to_all x8 -> x0, starting transfers between devices: 27.3 us -> none  [the longest x1 3.5 us: shards(): lax.all_to_all(grad_heads, 'head', split_axis=1, concat_axis=0, tiled=True)]
    pallas_call x0 -> x1, Pallas kernels: none -> 16.1 us  [shards(): pl.pallas_call(functools.partial(kernel, chips, reach, blk_size, group),...]
    all_to_all x1 -> x0, blocking collectives: 13.7 us -> none  [shards(): lax.all_to_all(row_delta, 'head', split_axis=1, concat_axis=0, tiled=True)]
    unnamed x14 -> x18, local copies, waits for them, and re-layouts: 1.42 us -> 6.09 us
    dot_general x13 -> x0, matrix products: 3.54 us -> none  [the longest x2 0.65 us: allowed_pairs(): reach_table = jnp.dot(reach_rows, key_hot.T, precision=top_precision)]
    while x7 -> x0, local copies, waits for them, and re-layouts: 2.7 us -> none  [the longest x3 2.66 us: shards(): final_state = lax.fori_loop(0, cycle_size, one_turn, start_state)]
    ppermute x8 -> x0, starting transfers between devices: 2.28 us -> none  [from_behind(): return lax.ppermute(value, axis, pairs)]
  transfers between devices with their start and end apart: 16 -> 0, of which waited for: 12 -> 0; matrix products, arithmetic and copies ran while one was open for 5% -> 0% of each run, Pallas kernels for 0% -> 0%
where the time goes in v1:
time: 23.2 us; the launch traced here: 22.8 us
  Pallas kernels  16.1 us (69%)
  local copies, waits for them, and re-layouts  6.09 us (26%)
  between operations  0.69 us (3%)
    pallas_call x1, Pallas kernels, shards(): pl.pallas_call(functools.partial(kernel, chips, reach, blk_size, group),...  16.1 us
    unnamed x18, local copies, waits for them, and re-layouts  6.09 us

profile of v1, /device:TPU:0, one launch (start us, length us, event | category | flops | bytes accessed | tf_op | source)
XLA Modules:
  0.0 22.8 jit_solution(10145529939736931610)
XLA Ops:
  0.6 0.0 copy-start.6
  0.6 0.0 copy-start.5
  0.7 0.0 copy-start.3
  0.7 0.8 %copy.11.l_hbm = f32[32,16]{1,0:T(8,128)S(1)} copy(f32[32,16]{0,1:T(8,128)} %param.13) | data formatting | bytes 4096 | tf_op args[5]
  1.4 0.0 copy-done.6
  1.5 0.0 copy-done.5
  1.5 0.0 copy-done.3
  1.5 0.0 copy-start
  1.5 0.9 %copy-done = bf16[32,2048]{1,0:T(8,128)(2,1)S(1)} copy-done((bf16[32,2048]{1,0:T(8,128)(2,1)S(1)}, bf16[32,2048]{1,0:T(8,128)(2,1)}, u32[]{:S(2)}) %copy-start) | copy-done | bytes 131096
  2.4 0.0 copy-start.1
  2.4 0.9 %copy-done.1 = bf16[32,2048]{1,0:T(8,128)(2,1)S(1)} copy-done((bf16[32,2048]{1,0:T(8,128)(2,1)S(1)}, bf16[32,2048]{1,0:T(8,128)(2,1)}, u32[]{:S(2)}) %copy-start.1) | copy-done | bytes 131096
  3.3 0.0 copy-start.2
  3.3 0.9 %copy-done.2 = bf16[32,2048]{1,0:T(8,128)(2,1)S(1)} copy-done((bf16[32,2048]{1,0:T(8,128)(2,1)S(1)}, bf16[32,2048]{1,0:T(8,128)(2,1)}, u32[]{:S(2)}) %copy-start.2) | copy-done | bytes 131096
  4.2 0.0 copy-start.4
  4.2 0.7 %copy-done.4 = bf16[32,256]{1,0:T(8,128)(2,1)S(1)} copy-done((bf16[32,256]{1,0:T(8,128)(2,1)S(1)}, bf16[32,256]{1,0:T(8,128)(2,1)}, u32[]{:S(2)}) %copy-start.4) | copy-done | bytes 16408
  4.9 16.1 %shard_map.103 = (bf16[32,2048]{1,0:T(8,128)(2,1)S(1)}, bf16[32,256]{1,0:T(8,128)(2,1)S(1)}, bf16[32,256]{1,0:T(8,128)(2,1)S(1)}) custom-call(s32[4,4]{1,0:T(4,128)S(1)} %copy-done.5, s32[4]{0:T(128)S(1)} %copy-done.6, bf16[32,2048]{1,0:T(8,128)(2,1)S(1)} %copy-done, bf16[32,256]{1,0:T(8,128)(2,1)S(1)} %copy-done.3, bf16[32,256]{1,0:T(8,128)(2,1)S(1)} %copy-done.4, ...), custom_call_target="tpu_custom_call" | custom-call | tf_op jit(solution)/shard_map/pallas_call | solution.py:335
  21.0 0.7 %copy.15 = bf16[32,2048]{1,0:T(8,128)(2,1)} copy(bf16[32,2048]{1,0:T(8,128)(2,1)S(1)} %get-tuple-element.6) | data formatting | bytes 262144
  21.6 0.6 %copy.16 = bf16[32,256]{1,0:T(8,128)(2,1)} copy(bf16[32,256]{1,0:T(8,128)(2,1)S(1)} %get-tuple-element.7) | data formatting | bytes 32768
  22.2 0.6 %copy.17 = bf16[32,256]{1,0:T(8,128)(2,1)} copy(bf16[32,256]{1,0:T(8,128)(2,1)S(1)} %get-tuple-element.8) | data formatting | bytes 32768
Async XLA Ops:
  0.6 0.8 %copy-start.6 = (s32[4]{0:T(128)S(1)}, s32[4]{0:T(128)}, u32[]{:S(2)}) copy-start(s32[4]{0:T(128)} %seg_ref.1) | copy-start | bytes 52
  0.6 0.8 %copy-start.5 = (s32[4,4]{1,0:T(4,128)S(1)}, s32[4,4]{1,0:T(4,128)}, u32[]{:S(2)}) copy-start(s32[4,4]{1,0:T(4,128)} %vis_ref.1) | copy-start | bytes 196
  0.7 0.8 %copy-start.3 = (bf16[32,256]{1,0:T(8,128)(2,1)S(1)}, bf16[32,256]{1,0:T(8,128)(2,1)}, u32[]{:S(2)}) copy-start(bf16[32,256]{1,0:T(8,128)(2,1)} %k_hbm.1) | copy-start | bytes 49156
  1.5 0.9 %copy-start = (bf16[32,2048]{1,0:T(8,128)(2,1)S(1)}, bf16[32,2048]{1,0:T(8,128)(2,1)}, u32[]{:S(2)}) copy-start(bf16[32,2048]{1,0:T(8,128)(2,1)} %q_hbm.1) | copy-start | bytes 393220
  2.4 0.9 %copy-start.1 = (bf16[32,2048]{1,0:T(8,128)(2,1)S(1)}, bf16[32,2048]{1,0:T(8,128)(2,1)}, u32[]{:S(2)}) copy-start(bf16[32,2048]{1,0:T(8,128)(2,1)} %o_hbm.1) | copy-start | bytes 393220
  3.3 0.9 %copy-start.2 = (bf16[32,2048]{1,0:T(8,128)(2,1)S(1)}, bf16[32,2048]{1,0:T(8,128)(2,1)}, u32[]{:S(2)}) copy-start(bf16[32,2048]{1,0:T(8,128)(2,1)} %g_hbm.1) | copy-start | bytes 393220
  4.2 0.7 %copy-start.4 = (bf16[32,256]{1,0:T(8,128)(2,1)S(1)}, bf16[32,256]{1,0:T(8,128)(2,1)}, u32[]{:S(2)}) copy-start(bf16[32,256]{1,0:T(8,128)(2,1)} %v_hbm.1) | copy-start | bytes 49156

commit v2 on v1

--- a/solution.py
+++ b/solution.py
@@ -31,7 +31,8 @@
 def kernel(
     chips, reach, blk_size, group,
     vis_ref, seg_ref, q_hbm, k_hbm, v_hbm, o_hbm, g_hbm, l_hbm,
-    dq_ref, dk_ref, dv_ref,
+    dq_hbm, dk_hbm, dv_hbm,
+    dq_ref, dk_ref, dv_ref, out_sem,
     q_in, k_in, v_in, o_in, g_in, l_in, in_sem,
     rows, rows_out, kv_out, kv, ds_all, part, back, own_part, dq_out, dq_back,
     x_send, x_recv, kv_send, kv_recv, part_send, part_recv, dq_send, dq_recv,
@@ -76,12 +77,43 @@
     on_chips(1, reach + 1, 1, greet)
     on_chips(1, reach + 1, -1, greet)
 
-    loads[0].wait()
-    loads[1].wait()
+    for load in loads:
+        load.wait()
     for c in range(CORES):
         kv_out[c, 0] = k_in[:, c * dh : (c + 1) * dh]
         kv_out[c, 1] = v_in[:, c * dh : (c + 1) * dh]
     kv[0, pl.ds(core, 1)] = kv_out[pl.ds(core, 1)]
+
+    lane = lax.broadcasted_iota(jnp.int32, (tok, dh), 1)
+
+    lse_in = jnp.transpose(l_in[...])
+
+    def prepare(column):
+        at_h = pl.ds(pl.multiple_of(column * dh, dh), dh)
+        g_h = g_in[:, at_h]
+        delta = jnp.sum(g_h.astype(jnp.float32) * o_in[:, at_h].astype(jnp.float32), axis=1, keepdims=True)
+        return at_h, g_h, delta
+
+    def extra(lse, delta):
+        value = jnp.where(lane < 3, lse * (1.0 / scale), jnp.where(lane < 6, delta, 0.0))
+        high = value.astype(jnp.bfloat16).astype(jnp.float32)
+        rest = value - high
+        middle = rest.astype(jnp.bfloat16).astype(jnp.float32)
+        third = (lane == 0) | (lane == 3)
+        second = (lane == 1) | (lane == 4)
+        return jnp.where(third, high, jnp.where(second, middle, rest - middle)).astype(jnp.bfloat16)
+
+    def fill(target, mine):
+        base = mine * group
+        lse_all = jnp.where(mine == 0, lse_in[:, :group], lse_in[:, group:])
+        for h in range(group):
+            at_h, g_h, delta = prepare(base + h)
+            r = slice(h * tok, (h + 1) * tok)
+            target[0, r] = q_in[:, at_h]
+            target[1, r] = extra(lse_all[:, h : h + 1], delta)
+            target[2, r] = g_h
+
+    fill(rows_out, other)
 
     near = jnp.minimum(chip, reach) + jnp.minimum(chips - 1 - chip, reach)
     pl.semaphore_wait(barrier, CORES * near + 1)
@@ -113,37 +145,6 @@
     on_chips(1, reach + 1, 1, send_kv)
     kv_copy(0, chip, other).start()
 
-    for load in loads[2:]:
-        load.wait()
-
-    lane = lax.broadcasted_iota(jnp.int32, (tok, dh), 1)
-
-    def prepare(h, column):
-        at_h = pl.ds(pl.multiple_of(column * dh, dh), dh)
-        g_h = g_in[:, at_h]
-        delta = jnp.sum(g_h.astype(jnp.float32) * o_in[:, at_h].astype(jnp.float32), axis=1, keepdims=True)
-        return at_h, g_h, delta
-
-    def extra(lse, delta):
-        value = jnp.where(lane < 3, lse * (1.0 / scale), jnp.where(lane < 6, delta, 0.0))
-        high = value.astype(jnp.bfloat16).astype(jnp.float32)
-        rest = value - high
-        middle = rest.astype(jnp.bfloat16).astype(jnp.float32)
-        third = (lane == 0) | (lane == 3)
-        second = (lane == 1) | (lane == 4)
-        return jnp.where(third, high, jnp.where(second, middle, rest - middle)).astype(jnp.bfloat16)
-
-    def fill(target, mine):
-        base = mine * group
-        lse_all = jnp.where(mine == 0, l_in[:, :group], l_in[:, group:])
-        for h in range(group):
-            at_h, g_h, delta = prepare(h, base + h)
-            r = slice(h * tok, (h + 1) * tok)
-            target[0, r] = q_in[:, at_h]
-            target[1, r] = extra(lse_all[:, h : h + 1], delta)
-            target[2, r] = g_h
-
-    fill(rows_out, other)
     x_copy = pltpu.make_async_remote_copy(
         src_ref=rows_out,
         dst_ref=rows.at[core],
@@ -282,6 +283,12 @@
         r = slice(h * tok, (h + 1) * tok)
         dq_ref[:, pl.ds(pl.multiple_of((other * group + h) * dh, dh), dh)] = dq_back[r]
 
+    stores = [
+        pltpu.make_async_copy(src, dst, out_sem.at[i])
+        for i, (src, dst) in enumerate(((dq_ref, dq_hbm), (dk_ref, dk_hbm), (dv_ref, dv_hbm)))
+    ]
+    stores[0].start()
+
     part_arrived(0, chip, other)
     for c in range(CORES):
         for which in range(2):
@@ -296,6 +303,8 @@
     for c in range(CORES):
         dk_ref[:, c * dh : (c + 1) * dh] = own_part[c, 0].astype(jnp.bfloat16)
         dv_ref[:, c * dh : (c + 1) * dh] = own_part[c, 1].astype(jnp.bfloat16)
+    stores[1].start()
+    stores[2].start()
 
     x_copy.wait_send()
     dq_copy.wait_send()
@@ -312,6 +321,19 @@
 
     on_chips(1, reach + 1, 1, kv_left)
     on_chips(1, reach + 1, -1, part_left)
+    for copy in stores:
+        copy.wait()
+
+
+def store(a_in, b_in, c_in, a_out, b_out, c_out, sem):
+    copies = [
+        pltpu.make_async_copy(src, dst, sem.at[i])
+        for i, (src, dst) in enumerate(((a_in, a_out), (b_in, b_out), (c_in, c_out)))
+    ]
+    for copy in copies:
+        copy.start()
+    for copy in copies:
+        copy.wait()
 
 
 def solution(mesh):
@@ -332,7 +354,7 @@
         bf16, f32 = jnp.bfloat16, jnp.float32
         slots = reach + 1
         dma = pltpu.SemaphoreType.DMA
-        return pl.pallas_call(
+        grads = pl.pallas_call(
             functools.partial(kernel, chips, reach, blk_size, group),
             out_shape=(
                 jax.ShapeDtypeStruct(queries.shape, bf16),
@@ -340,15 +362,19 @@
                 jax.ShapeDtypeStruct(value_rows.shape, bf16),
             ),
             in_specs=[pl.BlockSpec(memory_space=pltpu.SMEM)] * 2
-            + [pl.BlockSpec(memory_space=pl.ANY)] * 6,
-            out_specs=[pl.BlockSpec(memory_space=pltpu.VMEM)] * 3,
+            + [pl.BlockSpec(memory_space=pltpu.HBM)] * 6,
+            out_specs=[pl.BlockSpec(memory_space=pltpu.HBM)] * 3,
             scratch_shapes=[
+                pltpu.VMEM(queries.shape, bf16),
+                pltpu.VMEM(key_rows.shape, bf16),
+                pltpu.VMEM(value_rows.shape, bf16),
+                dma((3,)),
                 pltpu.VMEM(queries.shape, bf16),
                 pltpu.VMEM(key_rows.shape, bf16),
                 pltpu.VMEM(value_rows.shape, bf16),
                 pltpu.VMEM(fwd_output.shape, bf16),
                 pltpu.VMEM(grad_out.shape, bf16),
-                pltpu.VMEM(log_norm.shape, f32),
+                pltpu.VMEM(log_norm.shape[::-1], f32),
                 dma((6,)),
                 pltpu.VMEM((CORES, 3, n_rows, dh), bf16),
                 pltpu.VMEM((3, n_rows, dh), bf16),
@@ -366,9 +392,17 @@
                 dma, dma,
             ],
             compiler_params=pltpu.CompilerParams(
-                collective_id=0, has_side_effects=True, vmem_limit_bytes=48 << 20
+                collective_id=0, has_side_effects=True, vmem_limit_bytes=56 << 20
             ),
-        )(visible, seg_lengths, queries, key_rows, value_rows, fwd_output, grad_out, log_norm)
+        )(visible, seg_lengths, queries, key_rows, value_rows, fwd_output, grad_out, log_norm.T)
+
+        return pl.pallas_call(
+            store,
+            out_shape=[jax.ShapeDtypeStruct(g.shape, g.dtype) for g in grads],
+            in_specs=[pl.BlockSpec(memory_space=pltpu.HBM)] * 3,
+            out_specs=[pl.BlockSpec(memory_space=pltpu.HBM)] * 3,
+            scratch_shapes=[dma((3,))],
+        )(*grads)
 
     tokens = P(("groups", "head", "blk"), None)
     return jax.shard_map(

time: 23.2 us -> 23.3 us (level)
  Pallas kernels: 16.1 us -> 22.3 us
  local copies, waits for them, and re-layouts: 6.09 us -> 0 us
    pallas_call x0 -> x1, Pallas kernels: none -> 6.09 us  [shards(): pl.pallas_call(store, out_shape=[jax.ShapeDtypeStruct(g.shape, g.dtype) f...]
    unnamed x18 -> x0, local copies, waits for them, and re-layouts: 6.09 us -> none
where the time goes in v2:
time: 23.3 us; the launch traced here: 23 us
  Pallas kernels  22.3 us (96%)
  between operations  0.64 us (3%)
    pallas_call x1, Pallas kernels, shards(): pl.pallas_call(functools.partial(kernel, chips, reach, blk_size, group),...  16.2 us
    pallas_call x1, Pallas kernels, shards(): pl.pallas_call(store, out_shape=[jax.ShapeDtypeStruct(g.shape, g.dtype) f...  6.09 us

profile of v2, /device:TPU:0, one launch (start us, length us, event | category | flops | bytes accessed | tf_op | source)
XLA Modules:
  0.0 23.0 jit_solution(10350180247310173485)
XLA Ops:
  0.6 16.2 %shard_map.103 = (bf16[32,2048]{1,0:T(8,128)(2,1)}, bf16[32,256]{1,0:T(8,128)(2,1)}, bf16[32,256]{1,0:T(8,128)(2,1)}) custom-call(s32[4,4]{1,0:T(4,128)} %vis_ref.1, s32[4]{0:T(128)} %seg_ref.1, bf16[32,2048]{1,0:T(8,128)(2,1)} %q_hbm.1, bf16[32,256]{1,0:T(8,128)(2,1)} %k_hbm.1, bf16[32,256]{1,0:T(8,128)(2,1)} %v_hbm.1, bf16[32,2048]{1,0:T(8,128)(2,1)} %o_hbm.1, ...), custom_call_target="tpu_custom_call" | custom-call | tf_op jit(solution)/shard_map/pallas_call | solution.py:357
  16.9 6.1 %shard_map.104 = (bf16[32,2048]{1,0:T(8,128)(2,1)}, bf16[32,256]{1,0:T(8,128)(2,1)}, bf16[32,256]{1,0:T(8,128)(2,1)}) custom-call(bf16[32,2048]{1,0:T(8,128)(2,1)} %get-tuple-element.6.a_in, bf16[32,256]{1,0:T(8,128)(2,1)} %get-tuple-element.7.b_in, bf16[32,256]{1,0:T(8,128)(2,1)} %get-tuple-element.8.c_in), custom_call_target="tpu_custom_call" | custom-call | tf_op jit(solution)/shard_map/pallas_call | solution.py:399

commit v3 on v2

--- a/solution.py
+++ b/solution.py
@@ -20,9 +20,9 @@
     return lax.dot_general(a, b, dims, preferred_element_type=jnp.float32)
 
 
-def each(first, last, body):
+def each(first, last, body, down=False):
     if last - first <= 8:
-        for k in range(first, last):
+        for k in range(last - 1, first - 1, -1) if down else range(first, last):
             body(k)
     else:
         lax.fori_loop(first, last, lambda k, c: (body(k), c)[1], 0)
@@ -30,10 +30,9 @@
 
 def kernel(
     chips, reach, blk_size, group,
-    vis_ref, seg_ref, q_hbm, k_hbm, v_hbm, o_hbm, g_hbm, l_hbm,
-    dq_hbm, dk_hbm, dv_hbm,
-    dq_ref, dk_ref, dv_ref, out_sem,
-    q_in, k_in, v_in, o_in, g_in, l_in, in_sem,
+    vis_hbm, seg_hbm, q_hbm, k_hbm, v_hbm, o_hbm, g_hbm, l_hbm,
+    dq_ref, dk_ref, dv_ref,
+    vis_ref, seg_ref, q_in, k_in, v_in, o_in, g_in, l_in, in_sem,
     rows, rows_out, kv_out, kv, ds_all, part, back, own_part, dq_out, dq_back,
     x_send, x_recv, kv_send, kv_recv, part_send, part_recv, dq_send, dq_recv,
 ):
@@ -49,7 +48,7 @@
         where = its_chip * CORES + its_core
         return {"head": where // blk_size, "blk": where % blk_size}
 
-    def on_chips(first, last, sign, body):
+    def on_chips(first, last, sign, body, down=False):
         def one(k):
             its_chip = chip + sign * k
 
@@ -57,7 +56,7 @@
             def _():
                 body(k, its_chip)
 
-        each(first, last, one)
+        each(first, last, one, down)
 
     barrier = pltpu.get_barrier_semaphore()
 
@@ -68,7 +67,8 @@
     loads = [
         pltpu.make_async_copy(src, dst, in_sem.at[i])
         for i, (src, dst) in enumerate(
-            ((k_hbm, k_in), (v_hbm, v_in), (q_hbm, q_in), (g_hbm, g_in), (o_hbm, o_in), (l_hbm, l_in))
+            ((k_hbm, k_in), (v_hbm, v_in), (q_hbm, q_in), (g_hbm, g_in), (o_hbm, o_in), (l_hbm, l_in),
+             (vis_hbm, vis_ref), (seg_hbm, seg_ref))
         )
     ]
     for load in loads:
@@ -142,7 +142,7 @@
         for c in range(CORES):
             kv_copy(k, its_chip, c).start()
 
-    on_chips(1, reach + 1, 1, send_kv)
+    on_chips(1, reach + 1, 1, send_kv, True)
     kv_copy(0, chip, other).start()
 
     x_copy = pltpu.make_async_remote_copy(
@@ -245,7 +245,7 @@
             kv[k] = jnp.zeros(kv.shape[1:], kv.dtype)
             ds_all[k] = jnp.zeros(ds_all.shape[1:], ds_all.dtype)
 
-    each(1, reach + 1, one_chunk)
+    each(1, reach + 1, one_chunk, True)
 
     total = reach + 1
     at_once = max(n for n in range(1, 9) if total % n == 0)
@@ -283,12 +283,6 @@
         r = slice(h * tok, (h + 1) * tok)
         dq_ref[:, pl.ds(pl.multiple_of((other * group + h) * dh, dh), dh)] = dq_back[r]
 
-    stores = [
-        pltpu.make_async_copy(src, dst, out_sem.at[i])
-        for i, (src, dst) in enumerate(((dq_ref, dq_hbm), (dk_ref, dk_hbm), (dv_ref, dv_hbm)))
-    ]
-    stores[0].start()
-
     part_arrived(0, chip, other)
     for c in range(CORES):
         for which in range(2):
@@ -303,8 +297,6 @@
     for c in range(CORES):
         dk_ref[:, c * dh : (c + 1) * dh] = own_part[c, 0].astype(jnp.bfloat16)
         dv_ref[:, c * dh : (c + 1) * dh] = own_part[c, 1].astype(jnp.bfloat16)
-    stores[1].start()
-    stores[2].start()
 
     x_copy.wait_send()
     dq_copy.wait_send()
@@ -321,8 +313,6 @@
 
     on_chips(1, reach + 1, 1, kv_left)
     on_chips(1, reach + 1, -1, part_left)
-    for copy in stores:
-        copy.wait()
 
 
 def store(a_in, b_in, c_in, a_out, b_out, c_out, sem):
@@ -361,21 +351,18 @@
                 jax.ShapeDtypeStruct(key_rows.shape, bf16),
                 jax.ShapeDtypeStruct(value_rows.shape, bf16),
             ),
-            in_specs=[pl.BlockSpec(memory_space=pltpu.SMEM)] * 2
-            + [pl.BlockSpec(memory_space=pltpu.HBM)] * 6,
-            out_specs=[pl.BlockSpec(memory_space=pltpu.HBM)] * 3,
+            in_specs=[pl.BlockSpec(memory_space=pltpu.HBM)] * 8,
+            out_specs=[pl.BlockSpec(memory_space=pltpu.VMEM)] * 3,
             scratch_shapes=[
-                pltpu.VMEM(queries.shape, bf16),
-                pltpu.VMEM(key_rows.shape, bf16),
-                pltpu.VMEM(value_rows.shape, bf16),
-                dma((3,)),
+                pltpu.SMEM(visible.shape, jnp.int32),
+                pltpu.SMEM(seg_lengths.shape, jnp.int32),
                 pltpu.VMEM(queries.shape, bf16),
                 pltpu.VMEM(key_rows.shape, bf16),
                 pltpu.VMEM(value_rows.shape, bf16),
                 pltpu.VMEM(fwd_output.shape, bf16),
                 pltpu.VMEM(grad_out.shape, bf16),
                 pltpu.VMEM(log_norm.shape[::-1], f32),
-                dma((6,)),
+                dma((8,)),
                 pltpu.VMEM((CORES, 3, n_rows, dh), bf16),
                 pltpu.VMEM((3, n_rows, dh), bf16),
                 pltpu.VMEM((CORES, 2, tok, dh), bf16),
@@ -392,16 +379,22 @@
                 dma, dma,
             ],
             compiler_params=pltpu.CompilerParams(
-                collective_id=0, has_side_effects=True, vmem_limit_bytes=56 << 20
+                collective_id=0, has_side_effects=True, vmem_limit_bytes=48 << 20
             ),
-        )(visible, seg_lengths, queries, key_rows, value_rows, fwd_output, grad_out, log_norm.T)
+        )(
+            *(
+                pltpu.with_memory_space_constraint(x, pltpu.HBM)
+                for x in (visible, seg_lengths, queries, key_rows, value_rows, fwd_output, grad_out, log_norm.T)
+            ),
+        )
 
         return pl.pallas_call(
             store,
             out_shape=[jax.ShapeDtypeStruct(g.shape, g.dtype) for g in grads],
-            in_specs=[pl.BlockSpec(memory_space=pltpu.HBM)] * 3,
+            in_specs=[pl.BlockSpec(memory_space=pltpu.VMEM)] * 3,
             out_specs=[pl.BlockSpec(memory_space=pltpu.HBM)] * 3,
             scratch_shapes=[dma((3,))],
+            compiler_params=pltpu.CompilerParams(vmem_limit_bytes=1 << 20),
         )(*grads)
 
     tokens = P(("groups", "head", "blk"), None)

time: 23.3 us -> 15.3 us (0.66)
  the two profiles are of different devices: /device:TPU:0 before, /device:TPU:11 now
where the time goes in v3:
time: 15.3 us; the launch traced here: 15 us
  Pallas kernels  14.4 us (94%)
  between operations  0.64 us (4%)
    pallas_call x1, Pallas kernels, shards(): pl.pallas_call(functools.partial(kernel, chips, reach, blk_size, group),...  13.7 us
    pallas_call x1, Pallas kernels, shards(): pl.pallas_call(store, out_shape=[jax.ShapeDtypeStruct(g.shape, g.dtype) f...  0.69 us

profile of v3, /device:TPU:11, one launch (start us, length us, event | category | flops | bytes accessed | tf_op | source)
XLA Modules:
  0.0 15.0 jit_solution(4071930665445813568)
XLA Ops:
  0.6 13.7 %shard_map.103 = (bf16[32,2048]{1,0:T(8,128)(2,1)S(1)}, bf16[32,256]{1,0:T(8,128)(2,1)S(1)}, bf16[32,256]{1,0:T(8,128)(2,1)S(1)}) custom-call(s32[4,4]{1,0:T(4,128)} %vis_hbm.1, s32[4]{0:T(128)} %seg_hbm.1, bf16[32,2048]{1,0:T(8,128)(2,1)} %q_hbm.1, bf16[32,256]{1,0:T(8,128)(2,1)} %k_hbm.1, bf16[32,256]{1,0:T(8,128)(2,1)} %v_hbm.1, bf16[32,2048]{1,0:T(8,128)(2,1)} %o_hbm.1, ...), custom_call_target="tpu_custom_call" | custom-call | tf_op jit(solution)/shard_map/pallas_call | solution.py:347
  14.3 0.7 %shard_map.104 = (bf16[32,2048]{1,0:T(8,128)(2,1)}, bf16[32,256]{1,0:T(8,128)(2,1)}, bf16[32,256]{1,0:T(8,128)(2,1)}) custom-call(bf16[32,2048]{1,0:T(8,128)(2,1)S(1)} %get-tuple-element.6.a_in, bf16[32,256]{1,0:T(8,128)(2,1)S(1)} %get-tuple-element.7.b_in, bf16[32,256]{1,0:T(8,128)(2,1)S(1)} %get-tuple-element.8.c_in), custom_call_target="tpu_custom_call" | custom-call | tf_op jit(solution)/shard_map/pallas_call | solution.py:391

commit v4 on v3

--- a/solution.py
+++ b/solution.py
@@ -45,8 +45,10 @@
     other = 1 - core
 
     def at(its_chip, its_core):
-        where = its_chip * CORES + its_core
-        return {"head": where // blk_size, "blk": where % blk_size}
+        if blk_size == CORES:
+            return {"head": its_chip, "blk": its_core}
+        per_head = blk_size // CORES
+        return {"head": its_chip // per_head, "blk": its_chip % per_head * CORES + its_core}
 
     def on_chips(first, last, sign, body, down=False):
         def one(k):
@@ -71,18 +73,51 @@
              (vis_hbm, vis_ref), (seg_hbm, seg_ref))
         )
     ]
+    on_chips(1, reach + 1, -1, greet, True)
+    on_chips(1, reach + 1, 1, greet, True)
+    pl.semaphore_signal(barrier, inc=1, device_id=at(chip, other), device_id_type=MESH)
     for load in loads:
         load.start()
-    pl.semaphore_signal(barrier, inc=1, device_id=at(chip, other), device_id_type=MESH)
-    on_chips(1, reach + 1, 1, greet)
-    on_chips(1, reach + 1, -1, greet)
-
-    for load in loads:
-        load.wait()
+
+    loads[0].wait()
+    loads[1].wait()
     for c in range(CORES):
         kv_out[c, 0] = k_in[:, c * dh : (c + 1) * dh]
         kv_out[c, 1] = v_in[:, c * dh : (c + 1) * dh]
     kv[0, pl.ds(core, 1)] = kv_out[pl.ds(core, 1)]
+
+    near = jnp.minimum(chip, reach) + jnp.minimum(chips - 1 - chip, reach)
+    pl.semaphore_wait(barrier, CORES * near + 1)
+
+    def kv_copy(k, its_chip, its_core):
+        return pltpu.make_async_remote_copy(
+            src_ref=kv_out.at[its_core],
+            dst_ref=kv.at[k, core],
+            send_sem=kv_send.at[k, its_core],
+            recv_sem=kv_recv.at[k, core],
+            device_id=at(its_chip, its_core),
+            device_id_type=MESH,
+        )
+
+    def kv_arrived(k, its_chip, its_core):
+        pltpu.make_async_remote_copy(
+            src_ref=kv_out.at[0],
+            dst_ref=kv.at[k, its_core],
+            send_sem=kv_send.at[k, its_core],
+            recv_sem=kv_recv.at[k, its_core],
+            device_id=at(its_chip, its_core),
+            device_id_type=MESH,
+        ).wait_recv()
+
+    def send_kv(k, its_chip):
+        for c in range(CORES):
+            kv_copy(k, its_chip, c).start()
+
+    on_chips(1, reach + 1, 1, send_kv, True)
+    kv_copy(0, chip, other).start()
+
+    for load in loads[2:]:
+        load.wait()
 
     lane = lax.broadcasted_iota(jnp.int32, (tok, dh), 1)
 
@@ -114,37 +149,6 @@
             target[2, r] = g_h
 
     fill(rows_out, other)
-
-    near = jnp.minimum(chip, reach) + jnp.minimum(chips - 1 - chip, reach)
-    pl.semaphore_wait(barrier, CORES * near + 1)
-
-    def kv_copy(k, its_chip, its_core):
-        return pltpu.make_async_remote_copy(
-            src_ref=kv_out.at[its_core],
-            dst_ref=kv.at[k, core],
-            send_sem=kv_send.at[k, its_core],
-            recv_sem=kv_recv.at[k, core],
-            device_id=at(its_chip, its_core),
-            device_id_type=MESH,
-        )
-
-    def kv_arrived(k, its_chip, its_core):
-        pltpu.make_async_remote_copy(
-            src_ref=kv_out.at[0],
-            dst_ref=kv.at[k, its_core],
-            send_sem=kv_send.at[k, its_core],
-            recv_sem=kv_recv.at[k, its_core],
-            device_id=at(its_chip, its_core),
-            device_id_type=MESH,
-        ).wait_recv()
-
-    def send_kv(k, its_chip):
-        for c in range(CORES):
-            kv_copy(k, its_chip, c).start()
-
-    on_chips(1, reach + 1, 1, send_kv, True)
-    kv_copy(0, chip, other).start()
-
     x_copy = pltpu.make_async_remote_copy(
         src_ref=rows_out,
         dst_ref=rows.at[core],
@@ -223,12 +227,7 @@
             device_id_type=MESH,
         ).wait_recv()
 
-    kv_arrived(0, chip, other)
     x_copy.wait_recv()
-    grads(0, chip, True)
-    part_copy(0, chip, other).start()
-    back[0, pl.ds(core, 1)] = part[0, pl.ds(core, 1)]
-
     def one_chunk(k):
         its_chip = chip - k
 
@@ -246,26 +245,34 @@
             ds_all[k] = jnp.zeros(ds_all.shape[1:], ds_all.dtype)
 
     each(1, reach + 1, one_chunk, True)
+    kv_arrived(0, chip, other)
+    grads(0, chip, True)
+    part_copy(0, chip, other).start()
+    back[0, pl.ds(core, 1)] = part[0, pl.ds(core, 1)]
+
 
     total = reach + 1
     at_once = max(n for n in range(1, 9) if total % n == 0)
 
-    def query_part(first):
-        scores = jnp.concatenate([ds_all[first + i] for i in range(at_once)], axis=0)
+    def query_part(first, e):
+        mine = pl.ds(pl.multiple_of(e * n_rows, n_rows), n_rows)
+        scores = jnp.concatenate([ds_all[first + i, :, mine] for i in range(at_once)], axis=0)
         keys = jnp.concatenate(
-            [kv[first + i, e, 0] for i in range(at_once) for e in range(CORES)], axis=0
+            [kv[first + i, c, 0] for i in range(at_once) for c in range(CORES)], axis=0
         )
         return dot(scores, keys, TN)
 
-    if total == at_once:
-        query_grad = query_part(0)
-    else:
-        query_grad = lax.fori_loop(
-            0, total // at_once, lambda i, acc: acc + query_part(i * at_once),
-            jnp.zeros((CORES * n_rows, dh), jnp.float32),
-        )
-    for e in range(CORES):
-        dq_out[e] = query_grad[e * n_rows : (e + 1) * n_rows].astype(jnp.bfloat16)
+    def query_grad(e):
+        if total == at_once:
+            grad = query_part(0, e)
+        else:
+            grad = lax.fori_loop(
+                0, total // at_once, lambda i, acc: acc + query_part(i * at_once, e),
+                jnp.zeros((n_rows, dh), jnp.float32),
+            )
+        dq_out[e] = grad.astype(jnp.bfloat16)
+
+    query_grad(other)
     dq_copy = pltpu.make_async_remote_copy(
         src_ref=dq_out.at[other],
         dst_ref=dq_back,
@@ -275,6 +282,7 @@
         device_id_type=MESH,
     )
     dq_copy.start()
+    query_grad(core)
     for h in range(group):
         r = slice(h * tok, (h + 1) * tok)
         dq_ref[:, pl.ds(pl.multiple_of((core * group + h) * dh, dh), dh)] = dq_out[core, r]

time: 15.3 us -> 15.1 us (0.987)
  Pallas kernels: 14.4 us -> 14.2 us
    pallas_call x1, Pallas kernels: 13.7 us -> 13.5 us  [shards(): pl.pallas_call(functools.partial(kernel, chips, reach, blk_size, group),...]
where the time goes in v4:
time: 15.1 us; the launch traced here: 14.8 us
  Pallas kernels  14.2 us (94%)
  between operations  0.64 us (4%)
    pallas_call x1, Pallas kernels, shards(): pl.pallas_call(functools.partial(kernel, chips, reach, blk_size, group),...  13.5 us
    pallas_call x1, Pallas kernels, shards(): pl.pallas_call(store, out_shape=[jax.ShapeDtypeStruct(g.shape, g.dtype) f...  0.69 us

profile of v4, /device:TPU:11, one launch (start us, length us, event | category | flops | bytes accessed | tf_op | source)
XLA Modules:
  0.0 14.8 jit_solution(6450918863271792995)
XLA Ops:
  0.6 13.5 %shard_map.103 = (bf16[32,2048]{1,0:T(8,128)(2,1)S(1)}, bf16[32,256]{1,0:T(8,128)(2,1)S(1)}, bf16[32,256]{1,0:T(8,128)(2,1)S(1)}) custom-call(s32[4,4]{1,0:T(4,128)} %vis_hbm.1, s32[4]{0:T(128)} %seg_hbm.1, bf16[32,2048]{1,0:T(8,128)(2,1)} %q_hbm.1, bf16[32,256]{1,0:T(8,128)(2,1)} %k_hbm.1, bf16[32,256]{1,0:T(8,128)(2,1)} %v_hbm.1, bf16[32,2048]{1,0:T(8,128)(2,1)} %o_hbm.1, ...), custom_call_target="tpu_custom_call" | custom-call | tf_op jit(solution)/shard_map/pallas_call | solution.py:355
  14.1 0.7 %shard_map.104 = (bf16[32,2048]{1,0:T(8,128)(2,1)}, bf16[32,256]{1,0:T(8,128)(2,1)}, bf16[32,256]{1,0:T(8,128)(2,1)}) custom-call(bf16[32,2048]{1,0:T(8,128)(2,1)S(1)} %get-tuple-element.6.a_in, bf16[32,256]{1,0:T(8,128)(2,1)S(1)} %get-tuple-element.7.b_in, bf16[32,256]{1,0:T(8,128)(2,1)S(1)} %get-tuple-element.8.c_in), custom_call_target="tpu_custom_call" | custom-call | tf_op jit(solution)/shard_map/pallas_call | solution.py:399
